TPU v7x, 128 devices: a whole 4x4x4 slice. The times are simulated.
128 devices in a mesh: row: 8 (over x, core), col: 8 (over z_lo, y), mom: 2 (over z_hi).
Axes of the slice: x: 4, y: 4, z: 4 (z_hi: 2, z_lo: 2; z = z_hi * 2 + z_lo), core: 2. Of those that a mesh axis runs over, the one named last changes fastest.
Arguments:
- lesser: bfloat16 [4, 2, 3072, 3072], P('mom', None, 'row', 'col'), may hold values from -8 to 8
- greater: bfloat16 [4, 2, 3072, 3072], P('mom', None, 'col', 'row'), may hold values from -8 to 8
- triples: int32 [4, 8, 3], replicated, may hold values from 0 to 3
- diag_inverse: bfloat16 [4, 2, 3072, 384], P('mom', None, 'row'), may hold values from -0.21875 to 0.21875
- right_side: bfloat16 [4, 3072, 2, 3072], P('mom', 'row', None, 'col'), may hold values from -6 to 6
Outputs:
- sigma: bfloat16 [4, 2, 3072, 3072], P('mom', None, 'row', 'col')
- solution: bfloat16 [4, 3072, 2, 3072], P('mom', 'row', None, 'col')
Inputs may be any that keep to these rules, and one draw needn't show every extreme that they name: `triples`: each entry names a momentum point.
All inputs are finite; a program needn't handle non-finite values.
Results may differ from a plain program's by a relative error of at most 0.017.
Values may be sent and summed in bfloat16 or wider, within the bound.
A program may use at most 128 MiB of HBM per device.

v0:
```python
import math

import jax
import jax.numpy as jnp
from jax import lax
from jax.sharding import PartitionSpec as P


def broadcast(value, axis, source):
    kept = jnp.where(lax.axis_index(axis) == source, value, 0).astype(value.dtype)
    return lax.psum(kept, axis)


def complex_mul(left_real, left_imag, right_real, right_imag):
    return (
        left_real * right_real - left_imag * right_imag,
        left_real * right_imag + left_imag * right_real,
    )


def complex_product(left_tiles, right_rows):
    count = left_tiles.shape[0]
    height = left_tiles.shape[2]
    inner = left_tiles.shape[3]
    breadth = right_rows.shape[3]
    stacked = left_tiles.reshape(count, 2 * height, inner)
    spread = right_rows.reshape(count, inner, 2 * breadth)
    product = jnp.einsum("kab,kbc->kac", stacked, spread, preferred_element_type=jnp.float32)
    product = product.reshape(count, 2, height, 2, breadth)
    out_real = product[:, 0, :, 0] - product[:, 1, :, 1]
    out_imag = product[:, 0, :, 1] + product[:, 1, :, 0]
    return jnp.stack([out_real, out_imag], axis=2)


def on_device(lesser, greater, triples, diag_inverse, right_side):
    local_count = lesser.shape[0]
    lesser_all, greater_all = (
        lax.all_gather(lesser, "mom", axis=0, tiled=True),
        lax.all_gather(greater, "mom", axis=0, tiled=True),
    )
    partner_all = jnp.swapaxes(greater_all, 2, 3)
    first_moment = lax.axis_index("mom") * local_count
    pair_count = triples.shape[1]
    inv_pairs = 1.0 / pair_count

    def select_tile(stacked_tiles, which):
        return lax.dynamic_index_in_dim(stacked_tiles, which, 0, keepdims=False).astype(jnp.float32)

    sigma_parts = []
    for local_moment in range(local_count):
        table_rows = lax.dynamic_index_in_dim(
            triples, first_moment + local_moment, 0, keepdims=False
        )

        def add_term(pair_index, carry):
            sum_real, sum_imag = carry
            first_tile = select_tile(lesser_all, table_rows[pair_index, 0])
            second_tile = select_tile(lesser_all, table_rows[pair_index, 1])
            third_tile = select_tile(partner_all, table_rows[pair_index, 2])
            prod_real, prod_imag = complex_mul(
                first_tile[0], first_tile[1], second_tile[0], second_tile[1]
            )
            full_real, full_imag = complex_mul(prod_real, prod_imag, third_tile[0], third_tile[1])
            return (sum_real + full_real, sum_imag + full_imag)

        zero_tile = jnp.zeros(lesser.shape[2:], jnp.float32)
        sum_real, sum_imag = lax.fori_loop(0, pair_count, add_term, (zero_tile, zero_tile))
        sigma_parts.append(jnp.stack([sum_real, sum_imag]) * inv_pairs)
    sigma = jnp.stack(sigma_parts).astype(jnp.bfloat16)
    row_index = lax.axis_index("row")
    n_rows = lax.axis_size("row")
    tile_side = lesser.shape[2]
    weight = 1.0 / math.sqrt(tile_side * n_rows)
    kernel_rows = lax.all_gather(sigma, "col", axis=3, tiled=True)

    def solve_rows(pending):
        return complex_product(diag_inverse, pending.astype(jnp.bfloat16)).astype(jnp.bfloat16)

    def empty_rows(pending):
        return jnp.zeros(right_side.shape, jnp.bfloat16)

    def sweep(step_index, carry):
        pending, solved = carry
        is_owner = row_index == step_index
        candidate = lax.cond(is_owner, solve_rows, empty_rows, pending)
        solved = jnp.where(is_owner, candidate, solved)
        shared = broadcast(candidate, "row", step_index)
        kernel_tile = lax.dynamic_slice_in_dim(kernel_rows, step_index * tile_side, tile_side, 3)
        update = complex_product(kernel_tile, shared)
        pending = pending + jnp.where(row_index > step_index, weight * update, 0.0)
        return (pending, solved)

    start_pending = right_side.astype(jnp.float32)
    start_solved = jnp.zeros(right_side.shape, jnp.bfloat16)
    pending, solved = lax.fori_loop(0, n_rows - 1, sweep, (start_pending, start_solved))
    is_last = row_index == n_rows - 1
    last_rows = lax.cond(is_last, solve_rows, empty_rows, pending)
    solved = jnp.where(is_last, last_rows, solved)
    return (sigma, solved)


def solution(mesh):
    placed = (
        P("mom", None, "row", "col"),
        P("mom", None, "col", "row"),
        P(),
        P("mom", None, "row", None),
        P("mom", "row", None, "col"),
    )
    return jax.shard_map(
        on_device,
        mesh=mesh,
        in_specs=placed,
        out_specs=(P("mom", None, "row", "col"), P("mom", "row", None, "col")),
        check_vma=False,
    )
```

profile of v0, /device:TPU:23, one launch (start us, length us, event | category | flops | bytes accessed | tf_op | source)
XLA Modules:
  0.0 1176.0 jit_solution(3696177040927766123)
XLA Ops:
  8.8 43.1 %all-gather.6.cloned.1.call-done = bf16[4,2,384,384]{3,2,1,0:T(8,128)(2,1)} async-done(((bf16[2,2,384,384]{3,2,1,0:T(8,128)(2,1)}), bf16[4,2,384,384]{3,2,1,0:T(8,128)(2,1)}) %all-gather.6.cloned.1.call-update) | async-done | bytes 2359312 | tf_op jit(solution)/shard_map/all_gather | solution.py:39
  56.1 36.8 %all-gather.4.cloned.1.call-done = bf16[4,2,384,384]{3,2,1,0:T(8,128)(2,1)} async-done(((bf16[2,2,384,384]{3,2,1,0:T(8,128)(2,1)}), bf16[4,2,384,384]{3,2,1,0:T(8,128)(2,1)}) %all-gather.4.cloned.1.call-update) | async-done | bytes 2359312 | tf_op jit(solution)/shard_map/all_gather | solution.py:38
  93.0 92.0 %while.50 = (s32[]{:T(128)}, f32[384,384]{1,0:T(8,128)}, f32[384,384]{1,0:T(8,128)}, s32[8,3]{0,1:T(4,128)S(1)}, bf16[4,2,384,384]{3,2,1,0:T(8,128)(2,1)}, /*ind...) while((s32[]{:T(128)}, f32[384,384]{1,0:T(8,128)}, f32[384,384]{1,0:T(8,128)}, ...), condition=%wide.region_1.2_spmd.clone, body=%wide.region_0.1_spmd.clone.sunk | while | flops 3244044 | bytes 19464492 | solution.py:67
  185.0 91.5 %while.51 = (s32[]{:T(128)}, f32[384,384]{1,0:T(8,128)}, f32[384,384]{1,0:T(8,128)}, s32[8,3]{0,1:T(4,128)S(1)}, bf16[4,2,384,384]{3,2,1,0:T(8,128)(2,1)}, /*ind...) while((s32[]{:T(128)}, f32[384,384]{1,0:T(8,128)}, f32[384,384]{1,0:T(8,128)}, ...), condition=%wide.region_3.4_spmd.clone, body=%wide.region_2.3_spmd.clone.sunk | while | flops 3244044 | bytes 19464492 | solution.py:67
  281.4 96.6 %all-gather.8.cloned.1.call-done = bf16[2,2,384,3072]{3,2,1,0:T(8,128)(2,1)} async-done(((bf16[2,2,384,384]{3,2,1,0:T(8,128)(2,1)}), bf16[2,2,384,3072]{3,2,1,0:T(8,128)(2,1)}) %all-gather.8.cloned.1.call-update) | async-done | bytes 9437200 | tf_op jit(solution)/shard_map/all_gather | solution.py:74
  378.0 762.3 %while.52 = (s32[]{:T(128)}, f32[2,384,2,384]{3,2,1,0:T(2,128)S(1)}, bf16[2,384,2,384]{3,1,0,2:T(8,128)(2,1)}, s32[]{:T(128)}, bf16[2,2,384,3072]{3,2,1,0:T(8,12...) while((s32[]{:T(128)}, ...), condition=%wide.region_8.9_spmd.clone, body=%wide.region_4.8_spmd.clone.sunk | while | flops 1819607040 | bytes 87294256 | solution.py:95
  381.9 83.4 %all-reduce.2.cloned.1.call-done = bf16[2,384,768]{2,1,0:T(8,128)(2,1)} async-done(((bf16[2,384,768]{2,1,0:T(8,128)(2,1)}), bf16[2,384,768]{2,1,0:T(8,128)(2,1)}) %all-reduce.2.cloned.1.call-update) | async-done | bytes 1179664 | tf_op jit(solution)/shard_map/while/body/eval_jaxpr/psum | solution.py:11
  470.2 6.7 reshape.316
  476.9 6.0 fusion.33
  491.8 81.7 %all-reduce.2.cloned.1.call-done = bf16[2,384,768]{2,1,0:T(8,128)(2,1)} async-done(((bf16[2,384,768]{2,1,0:T(8,128)(2,1)}), bf16[2,384,768]{2,1,0:T(8,128)(2,1)}) %all-reduce.2.cloned.1.call-update) | async-done | bytes 1179664 | tf_op jit(solution)/shard_map/while/body/eval_jaxpr/psum | solution.py:11
  578.4 6.7 reshape.316
  585.1 6.0 fusion.33
  600.0 82.9 %all-reduce.2.cloned.1.call-done = bf16[2,384,768]{2,1,0:T(8,128)(2,1)} async-done(((bf16[2,384,768]{2,1,0:T(8,128)(2,1)}), bf16[2,384,768]{2,1,0:T(8,128)(2,1)}) %all-reduce.2.cloned.1.call-update) | async-done | bytes 1179664 | tf_op jit(solution)/shard_map/while/body/eval_jaxpr/psum | solution.py:11
  687.8 6.7 reshape.316
  694.5 6.0 fusion.33
  709.4 80.5 %all-reduce.2.cloned.1.call-done = bf16[2,384,768]{2,1,0:T(8,128)(2,1)} async-done(((bf16[2,384,768]{2,1,0:T(8,128)(2,1)}), bf16[2,384,768]{2,1,0:T(8,128)(2,1)}) %all-reduce.2.cloned.1.call-update) | async-done | bytes 1179664 | tf_op jit(solution)/shard_map/while/body/eval_jaxpr/psum | solution.py:11
  794.8 6.7 reshape.316
  801.5 6.0 fusion.33
  816.4 82.7 %all-reduce.2.cloned.1.call-done = bf16[2,384,768]{2,1,0:T(8,128)(2,1)} async-done(((bf16[2,384,768]{2,1,0:T(8,128)(2,1)}), bf16[2,384,768]{2,1,0:T(8,128)(2,1)}) %all-reduce.2.cloned.1.call-update) | async-done | bytes 1179664 | tf_op jit(solution)/shard_map/while/body/eval_jaxpr/psum | solution.py:11
  899.1 4.9 fusion.32
  904.0 6.7 reshape.316
  910.7 6.0 fusion.33
  925.6 82.9 %all-reduce.2.cloned.1.call-done = bf16[2,384,768]{2,1,0:T(8,128)(2,1)} async-done(((bf16[2,384,768]{2,1,0:T(8,128)(2,1)}), bf16[2,384,768]{2,1,0:T(8,128)(2,1)}) %all-reduce.2.cloned.1.call-update) | async-done | bytes 1179664 | tf_op jit(solution)/shard_map/while/body/eval_jaxpr/psum | solution.py:11
  1013.4 6.7 reshape.316
  1020.1 6.0 fusion.33
  1035.1 84.0 %all-reduce.2.cloned.1.call-done = bf16[2,384,768]{2,1,0:T(8,128)(2,1)} async-done(((bf16[2,384,768]{2,1,0:T(8,128)(2,1)}), bf16[2,384,768]{2,1,0:T(8,128)(2,1)}) %all-reduce.2.cloned.1.call-update) | async-done | bytes 1179664 | tf_op jit(solution)/shard_map/while/body/eval_jaxpr/psum | solution.py:11
  1119.1 4.9 fusion.32
  1124.0 6.7 reshape.316
  1130.7 6.0 fusion.33
  1140.3 25.1 %conditional.2 = (bf16[2,384,2,384]{3,2,1,0:T(2,128)(2,1)}) conditional(s32[]{:T(128)} %convert_element_type.81, () %tuple.72, (bf16[2,2,384,384]{3,2,1,0:T(8,128)(2,1)}, f32[2,384,2,384]{3,2,1,0:T(2,128)S(1)}) %tuple.184), branch_computations={%region_9.10_spmd, %region_10.11_spmd} | conditional | flops 908328960 | bytes 47185956 | solution.py:97
  1149.2 6.7 reshape.303
  1155.9 6.7 fusion.15
  (226 shorter events, 201.0 us)
Async XLA Ops:
  7.2 1.6 copy-start.9
  7.2 44.7 %all-gather.6.cloned.1.call-start = ((), (), s32[]{:S(2)}) async-start(), calls=%async_computation.1 | async-start | bytes 3538944 | tf_op jit(solution)/shard_map/all_gather | solution.py:39
  7.9 85.1 %all-gather.4.cloned.1.call-start = ((), (), s32[]{:S(2)}) async-start(), calls=%async_computation | async-start | bytes 3538944 | tf_op jit(solution)/shard_map/all_gather | solution.py:38
  8.7 369.3 %all-gather.8.cloned.1.call-start = ((), (), s32[]{:S(2)}) async-start(), calls=%async_computation.2 | async-start | bytes 10616832 | tf_op jit(solution)/shard_map/all_gather | solution.py:74
  101.2 1.1 copy-start.6
  111.7 2.2 copy-start.6
  123.3 2.2 copy-start.6
  135.0 2.2 copy-start.6
  146.6 2.2 copy-start.6
  158.3 2.2 copy-start.6
  169.9 2.2 copy-start.6
  181.5 2.2 copy-start.6
  193.1 1.1 copy-start.3
  203.6 2.2 copy-start.3
  215.2 2.2 copy-start.3
  226.8 2.2 copy-start.3
  238.3 2.2 copy-start.3
  249.9 2.2 copy-start.3
  261.5 2.2 copy-start.3
  273.1 2.2 copy-start.3
  276.5 1.4 copy-start.2
  276.5 1.6 copy-start.5
  279.3 1.3 copy-start.8
  378.0 87.3 %all-reduce.2.cloned.1.call-start = ((), (), s32[]{:S(2)}) async-start(), calls=%async_computation.3 | async-start | bytes 2359296 | tf_op jit(solution)/shard_map/while/body/eval_jaxpr/psum | solution.py:11
  486.5 87.0 %all-reduce.2.cloned.1.call-start = ((), (), s32[]{:S(2)}) async-start(), calls=%async_computation.3 | async-start | bytes 2359296 | tf_op jit(solution)/shard_map/while/body/eval_jaxpr/psum | solution.py:11
  594.7 88.2 %all-reduce.2.cloned.1.call-start = ((), (), s32[]{:S(2)}) async-start(), calls=%async_computation.3 | async-start | bytes 2359296 | tf_op jit(solution)/shard_map/while/body/eval_jaxpr/psum | solution.py:11
  704.1 85.8 %all-reduce.2.cloned.1.call-start = ((), (), s32[]{:S(2)}) async-start(), calls=%async_computation.3 | async-start | bytes 2359296 | tf_op jit(solution)/shard_map/while/body/eval_jaxpr/psum | solution.py:11
  811.1 88.0 %all-reduce.2.cloned.1.call-start = ((), (), s32[]{:S(2)}) async-start(), calls=%async_computation.3 | async-start | bytes 2359296 | tf_op jit(solution)/shard_map/while/body/eval_jaxpr/psum | solution.py:11
  920.3 88.2 %all-reduce.2.cloned.1.call-start = ((), (), s32[]{:S(2)}) async-start(), calls=%async_computation.3 | async-start | bytes 2359296 | tf_op jit(solution)/shard_map/while/body/eval_jaxpr/psum | solution.py:11
  1029.7 89.4 %all-reduce.2.cloned.1.call-start = ((), (), s32[]{:S(2)}) async-start(), calls=%async_computation.3 | async-start | bytes 2359296 | tf_op jit(solution)/shard_map/while/body/eval_jaxpr/psum | solution.py:11
  1140.3 25.1 %copy-start.1 = (bf16[2,384,2,384]{3,1,0,2:T(8,128)(2,1)S(1)}, bf16[2,384,2,384]{3,1,0,2:T(8,128)(2,1)}, u32[]{:S(2)}) copy-start(bf16[2,384,2,384]{3,1,0,2:T(8,128)(2,1)} %get-tuple-element.407) | copy-start | bytes 3538948
  1142.4 3.2 copy-start
  (16 other events, 13.2 us)
Sparse Core Ops, SparseCore 0:
  9.6 42.1 all-gather.5
  53.5 39.4 all-gather.3
  279.5 98.4 all-gather.7
  380.8 84.4 all-reduce.1
  490.5 82.9 all-reduce.1
  598.7 84.1 all-reduce.1
  708.1 81.7 all-reduce.1
  815.2 83.9 all-reduce.1
  924.3 84.1 all-reduce.1
  1033.7 85.3 all-reduce.1
where the time goes:
time: 1180 us
  waiting for transfers between devices  756 us (64%)
  other arithmetic  159 us (13%)
  local copies, waits for them, and re-layouts  114 us (10%)
  loops' own time  94.6 us (8%)
  matrix products  37.6 us (3%)
  between operations  14.2 us (1%)
    psum x7, waiting for transfers between devices, broadcast(): return lax.psum(kept, axis)  578 us
    all_gather x1, waiting for transfers between devices, on_device(): kernel_rows = lax.all_gather(sigma, 'col', axis=3, tiled=True)  96.6 us
    another operation x2, loops' own time, on_device(): lax.fori_loop(0, pair_count, add_term, (zero_tile, zero_tile))  93.7 us
    reshape x8, local copies, waits for them, and re-layouts, complex_product(): product = product.reshape(count, 2, height, 2, breadth)  53.8 us
    all_gather x1, waiting for transfers between devices, on_device(): lax.all_gather(greater, 'mom', axis=0, tiled=True)  43.1 us
    sub x8, other arithmetic, complex_product(): out_real = product[:, 0, :, 0] - product[:, 1, :, 1]  42.7 us
    add x32, other arithmetic, add_term(): return (sum_real + full_real, sum_imag + full_imag)  39 us
    dot_general x8, matrix products, complex_product(): jnp.einsum('kab,kbc->kac', stacked, spread, preferred_element_type=jnp.fl...  37.6 us
  transfers between devices with their start and end apart: 10, of which 10 were waited for; matrix products, arithmetic and copies ran while one was open for 1% of the time, Pallas kernels for 0%

commit v1 on v0

v1 whole, which is shorter than its diff:
```python
import math

import jax
import jax.numpy as jnp
from jax import lax
from jax.experimental import pallas as pl
from jax.experimental.pallas import tpu as pltpu
from jax.sharding import PartitionSpec as P

MESH = pl.DeviceIdType.MESH
SIDE = 384
WIDE = 2 * SIDE
CHUNKS = 3
PART = SIDE // CHUNKS
GROUPS = 3
LANES = 128
PAIRS = 8
SUB = 16


def expand(tall):
    real, imag = tall[:, :LANES], tall[:, LANES:]
    turned = jnp.concatenate([-imag, real], axis=1)
    return jnp.concatenate([tall, turned], axis=0)


def kernel(
    triples, lesser, greater, diag, right,
    sigma, solved,
    l0, l1, l2, g0, g1, g2, partner, own_sigma, rows_of, dbuf, rbuf, acc, sol,
    ex_s, ex_r, loc, zs, zr, ys, yr, ss, sr, rs, rr, dl, ds_, dr, xs, xr, os_, or_, out_s,
):
    lch, gch = (l0, l1, l2), (g0, g1, g2)
    row = lax.axis_index("row")
    col = lax.axis_index("col")
    mom = lax.axis_index("mom")
    x, core = row // 2, row % 2
    zl, y = col // 4, col % 4
    weight = 1.0 / math.sqrt(SIDE * 8)

    def at(x_, core_, y_, zl_):
        return (x_ * 2 + core_, zl_ * 4 + y_, mom)

    pair_dev = (row, col, 1 - mom)
    sibling = at(x, 1 - core, y, zl)
    zflip = at(x, core, y, 1 - zl)

    def y_dev(d):
        return at(x, core, (y + d) % 4, zl)

    def x_dev(d):
        return at(x + d, core, y, zl)

    def remote(src, dst, send, recv, dev):
        return pltpu.make_async_remote_copy(
            src_ref=src, dst_ref=dst, send_sem=send, recv_sem=recv, device_id=dev, device_id_type=MESH
        )

    barrier = pltpu.get_barrier_semaphore()
    peers = [pair_dev, sibling, zflip, at(x, 1 - core, y, 1 - zl)]
    peers += [y_dev(d) for d in (1, 2, 3)]
    peers += [at((x + d) % 4, core, y, zl) for d in (1, 2, 3)]
    for peer in peers:
        pl.semaphore_signal(barrier, inc=1, device_id=peer, device_id_type=MESH)
    pl.semaphore_wait(barrier, len(peers))

    needed = col < row
    early = jnp.logical_or(needed, x == 3)
    late = jnp.logical_not(early)

    def part(i):
        return pl.ds(i * PART, PART)

    mine = pl.ds(2 * mom, 2)

    def exchange(i):
        return (
            remote(lesser.at[:, :, part(i), :], lch[i].at[mine], ex_s.at[i, 0], ex_r.at[i, 0], pair_dev),
            remote(greater.at[:, :, :, part(i)], gch[i].at[mine], ex_s.at[i, 1], ex_r.at[i, 1], pair_dev),
        )

    def keep(i):
        return (
            pltpu.make_async_copy(lesser.at[:, :, part(i), :], lch[i].at[mine], loc.at[i, 0]),
            pltpu.make_async_copy(greater.at[:, :, :, part(i)], gch[i].at[mine], loc.at[i, 1]),
        )

    def start_exchange():
        for i in range(CHUNKS):
            for copy in exchange(i):
                copy.start()

    pl.when(early)(start_exchange)

    def right_self(m):
        return jnp.logical_and(core == zl, zl == m)

    def right_send(m):
        return remote(right.at[m], rbuf.at[core], rs.at[m], rr.at[core], at(x, zl, y, m))

    def right_keep(m):
        return pltpu.make_async_copy(right.at[m], rbuf.at[core], rr.at[core])

    for m in range(2):
        pl.when(right_self(m))(lambda m=m: right_keep(m).start())
        pl.when(jnp.logical_not(right_self(m)))(lambda m=m: right_send(m).start())

    def diag_keep(q):
        return pltpu.make_async_copy(diag.at[zl, q], dbuf.at[core, :, pl.ds(q * SIDE, SIDE)], dl.at[q])

    def diag_send(q):
        return remote(
            diag.at[zl, q], dbuf.at[core, :, pl.ds(q * SIDE, SIDE)], ds_.at[q], dr.at[q], sibling
        )

    for q in range(2):
        diag_keep(q).start()
        diag_send(q).start()
    for i in range(CHUNKS):
        for copy in keep(i):
            copy.start()

    def sigma_out(i, q):
        return pltpu.make_async_copy(
            own_sigma.at[:, part(i), pl.ds(q * SIDE, SIDE)], sigma.at[:, q, part(i), :], out_s.at[i, q]
        )

    def compute_sigma(i):
        for copy in exchange(i):
            copy.wait_recv()
        for copy in keep(i):
            copy.wait()

        def turn(k, carry):
            for q in range(2):
                for b in range(3):
                    rows = pl.ds(b * LANES, LANES)
                    partner[k, q, :, rows] = gch[i][k, q, rows, :].T
            return carry

        lax.fori_loop(0, 4, turn, 0)

        def block(s, carry):
            here = pl.ds(pl.multiple_of(s * SUB, SUB), SUB)
            there = pl.ds(pl.multiple_of(i * PART + s * SUB, SUB), SUB)
            for m in range(2):
                sum_real = jnp.zeros((SUB, SIDE), jnp.float32)
                sum_imag = jnp.zeros((SUB, SIDE), jnp.float32)
                for p in range(PAIRS):
                    base = (2 * mom + m) * (3 * PAIRS) + 3 * p
                    a, b, c = triples[base], triples[base + 1], triples[base + 2]
                    ar = lch[i][a, 0, here, :].astype(jnp.float32)
                    ai = lch[i][a, 1, here, :].astype(jnp.float32)
                    br = lch[i][b, 0, here, :].astype(jnp.float32)
                    bi = lch[i][b, 1, here, :].astype(jnp.float32)
                    cr = partner[c, 0, here, :].astype(jnp.float32)
                    ci = partner[c, 1, here, :].astype(jnp.float32)
                    pr = ar * br - ai * bi
                    pi = ar * bi + ai * br
                    sum_real += pr * cr - pi * ci
                    sum_imag += pr * ci + pi * cr
                sig_real = (sum_real * (1.0 / PAIRS)).astype(jnp.bfloat16)
                sig_imag = (sum_imag * (1.0 / PAIRS)).astype(jnp.bfloat16)
                own_sigma[m, there, 0:SIDE] = sig_real
                own_sigma[m, there, SIDE:WIDE] = sig_imag

                @pl.when(zl == m)
                def _():
                    rows_of[core, col, there, 0:SIDE] = sig_real
                    rows_of[core, col, there, SIDE:WIDE] = sig_imag
            return carry

        lax.fori_loop(0, PART // SUB, block, 0)
        for q in range(2):
            sigma_out(i, q).start()

    def hop(i):
        return remote(
            own_sigma.at[1 - zl, part(i), :], rows_of.at[core, col, part(i), :], zs.at[i], zr.at[i], zflip
        )

    other_col = (1 - zl) * 4 + y
    other_needed = other_col < row

    def hop_in(i):
        tile = rows_of.at[core, other_col, part(i), :]
        return remote(tile, tile, zs.at[i], zr.at[i], zflip)

    def y_send(t, i, d):
        j = col if t == 0 else other_col
        src = own_sigma.at[zl, part(i), :] if t == 0 else rows_of.at[core, j, part(i), :]
        return remote(src, rows_of.at[core, j, part(i), :], ys.at[t, i, d - 1], yr.at[j, i], y_dev(d))

    def side_send(j, i):
        tile = rows_of.at[core, j, part(i), :]
        return remote(tile, tile, ss.at[j, i], sr.at[j, i], sibling)

    def side_own(i):
        return remote(
            own_sigma.at[zl, part(i), :], rows_of.at[core, col, part(i), :], ss.at[col, i], sr.at[col, i], sibling
        )

    def side_in(j, i):
        tile = rows_of.at[1 - core, j, part(i), :]
        return remote(tile, tile, ss.at[j, i], sr.at[j, i], sibling)

    def gathered(i):
        for d in (1, 2, 3):
            for half in range(2):
                j = half * 4 + (y + d) % 4

                @pl.when(j < row)
                def _(j=j):
                    tile = rows_of.at[core, j, part(i), :]
                    remote(tile, tile, ss.at[j, i], yr.at[j, i], sibling).wait_recv()
                    side_send(j, i).start()

    for i in range(CHUNKS):
        @pl.when(early)
        def _(i=i):
            compute_sigma(i)

        @pl.when(needed)
        def _(i=i):
            hop(i).start()
            for d in (1, 3, 2):
                y_send(0, i, d).start()
            side_own(i).start()

        @pl.when(other_needed)
        def _(i=i):
            hop_in(i).wait_recv()
            for d in (1, 3, 2):
                y_send(1, i, d).start()
            side_send(other_col, i).start()

        if i:
            gathered(i - 1)
    gathered(CHUNKS - 1)
    pl.when(late)(start_exchange)

    for q in range(2):
        diag_keep(q).wait()
        dst = dbuf.at[1 - core, :, pl.ds(q * SIDE, SIDE)]
        remote(diag.at[zl, q], dst, ds_.at[q], dr.at[q], sibling).wait_recv()
    for q in range(2):
        from_self = jnp.logical_and(core == q, zl == core)

        @pl.when(from_self)
        def _(q=q):
            pltpu.make_async_copy(right.at[0], rbuf.at[q], rr.at[q]).wait()

        @pl.when(jnp.logical_not(from_self))
        def _(q=q):
            remote(right.at[0], rbuf.at[q], rs.at[0], rr.at[q], sibling).wait_recv()

    def sol_send(q, g, d):
        tile = sol.at[2 * x + q, g]
        return remote(tile, tile, xs.at[q, g, d - 1], xr.at[2 * x + q, g], x_dev(d))

    def out_self(q):
        return jnp.logical_and(core == q, zl == core)

    def out_send(q, g):
        return remote(
            sol.at[2 * x + q, g], solved.at[zl, g], os_.at[q, g], or_.at[zl, g], at(x, q, y, core)
        )

    def out_keep(q, g):
        return pltpu.make_async_copy(sol.at[2 * x + q, g], solved.at[zl, g], or_.at[zl, g])

    def side_wait(j, which):
        @pl.when(core != which)
        def _():
            for i in range(CHUNKS):
                side_in(j, i).wait_recv()

    def group(g, carry):
        for q in range(2):
            acc[q] = rbuf[q, g].astype(jnp.float32)

        def update(step, c):
            for t in range(2):
                j = 2 * step + t
                tile = sol.at[j, g]
                remote(tile, tile, xs.at[0, g, 0], xr.at[j, g], sibling).wait_recv()

                @pl.when(g == 0)
                def _(j=j):
                    side_wait(j, 0)
                    side_wait(j, 1)

                factor = expand(sol[j, g])
                for q in range(2):
                    acc[q] += weight * jnp.dot(
                        rows_of[q, j], factor, preferred_element_type=jnp.float32
                    )
            return c

        lax.fori_loop(0, x, update, 0)

        for q in range(2):
            answer = jnp.dot(
                dbuf[q], expand(acc[q].astype(jnp.bfloat16)), preferred_element_type=jnp.float32
            ).astype(jnp.bfloat16)
            sol[2 * x + q, g] = answer
            for d in (1, 2, 3):
                @pl.when(x + d < 4)
                def _(q=q, d=d):
                    sol_send(q, g, d).start()
            pl.when(out_self(q))(lambda q=q: out_keep(q, g).start())
            pl.when(jnp.logical_not(out_self(q)))(lambda q=q: out_send(q, g).start())
            if q == 0:
                @pl.when(g == 0)
                def _():
                    side_wait(2 * x, 1)

                acc[1] += weight * jnp.dot(
                    rows_of[1, 2 * x], expand(answer), preferred_element_type=jnp.float32
                )
        return carry

    lax.fori_loop(0, GROUPS, group, 0)

    @pl.when(late)
    def _():
        for i in range(CHUNKS):
            compute_sigma(i)

    for i in range(CHUNKS):
        for copy in exchange(i):
            copy.wait_send()
        for q in range(2):
            sigma_out(i, q).wait()

        @pl.when(needed)
        def _(i=i):
            hop(i).wait_send()
            for d in (1, 2, 3):
                y_send(0, i, d).wait_send()
            side_own(i).wait_send()

        @pl.when(other_needed)
        def _(i=i):
            for d in (1, 2, 3):
                y_send(1, i, d).wait_send()
            side_send(other_col, i).wait_send()

        for d in (1, 2, 3):
            for half in range(2):
                j = half * 4 + (y + d) % 4

                @pl.when(j < row)
                def _(j=j, i=i):
                    side_send(j, i).wait_send()
    for m in range(2):
        pl.when(jnp.logical_not(right_self(m)))(lambda m=m: right_send(m).wait_send())
    for q in range(2):
        diag_send(q).wait_send()
    for g in range(GROUPS):
        for q in range(2):
            for d in (1, 2, 3):
                @pl.when(x + d < 4)
                def _(q=q, g=g, d=d):
                    sol_send(q, g, d).wait_send()
            pl.when(jnp.logical_not(out_self(q)))(lambda q=q, g=g: out_send(q, g).wait_send())
        for m in range(2):
            from_self = jnp.logical_and(core == zl, zl == m)

            @pl.when(from_self)
            def _(m=m, g=g):
                pltpu.make_async_copy(sol.at[0, g], solved.at[m, g], or_.at[m, g]).wait()

            @pl.when(jnp.logical_not(from_self))
            def _(m=m, g=g):
                remote(sol.at[0, g], solved.at[m, g], os_.at[0, g], or_.at[m, g], sibling).wait_recv()


def on_device(lesser, greater, triples, diag_inverse, right_side):
    count = right_side.shape[0]
    right = right_side.reshape(count, SIDE, 2, GROUPS, LANES).transpose(0, 3, 1, 2, 4)
    right = right.reshape(count, GROUPS, SIDE, 2 * LANES)
    bf16, f32 = jnp.bfloat16, jnp.float32
    dma = pltpu.SemaphoreType.DMA
    hbm = pl.BlockSpec(memory_space=pl.ANY)
    sigma, solved = pl.pallas_call(
        kernel,
        out_shape=(
            jax.ShapeDtypeStruct(lesser.shape, bf16),
            jax.ShapeDtypeStruct(right.shape, bf16),
        ),
        in_specs=[pl.BlockSpec(memory_space=pltpu.SMEM), hbm, hbm, hbm, hbm],
        out_specs=(hbm, hbm),
        scratch_shapes=[pltpu.VMEM((4, 2, PART, SIDE), bf16) for _ in range(CHUNKS)]
        + [pltpu.VMEM((4, 2, SIDE, PART), bf16) for _ in range(CHUNKS)]
        + [
            pltpu.VMEM((4, 2, PART, SIDE), bf16),
            pltpu.VMEM((2, SIDE, WIDE), bf16),
            pltpu.VMEM((2, 8, SIDE, WIDE), bf16),
            pltpu.VMEM((2, SIDE, WIDE), bf16),
            pltpu.VMEM((2, GROUPS, SIDE, 2 * LANES), bf16),
            pltpu.VMEM((2, SIDE, 2 * LANES), f32),
            pltpu.VMEM((8, GROUPS, SIDE, 2 * LANES), bf16),
            dma((CHUNKS, 2)), dma((CHUNKS, 2)), dma((CHUNKS, 2)),
            dma((CHUNKS,)), dma((CHUNKS,)),
            dma((2, CHUNKS, 3)), dma((8, CHUNKS)),
            dma((8, CHUNKS)), dma((8, CHUNKS)),
            dma((2,)), dma((2,)),
            dma((2,)), dma((2,)), dma((2,)),
            dma((2, GROUPS, 3)), dma((8, GROUPS)),
            dma((2, GROUPS)), dma((2, GROUPS)),
            dma((CHUNKS, 2)),
        ],
        compiler_params=pltpu.CompilerParams(
            collective_id=0, has_side_effects=True, vmem_limit_bytes=56 * 1024 * 1024
        ),
        name="second_born",
    )(triples.reshape(-1), lesser, greater, diag_inverse, right)
    solved = solved.reshape(count, GROUPS, SIDE, 2, LANES).transpose(0, 2, 3, 1, 4)
    return (sigma, solved.reshape(right_side.shape))


def solution(mesh):
    placed = (
        P("mom", None, "row", "col"),
        P("mom", None, "col", "row"),
        P(),
        P("mom", None, "row", None),
        P("mom", "row", None, "col"),
    )
    return jax.shard_map(
        on_device,
        mesh=mesh,
        in_specs=placed,
        out_specs=(P("mom", None, "row", "col"), P("mom", "row", None, "col")),
        check_vma=False,
    )
```

time: 1180 us -> 186 us (0.16)
  the two profiles are of different devices: /device:TPU:23 before, /device:TPU:21 now
where the time goes in v1:
time: 186 us
  Pallas kernels  170 us (91%)
  local copies, waits for them, and re-layouts  15.7 us (8%)
    pallas_call x1, Pallas kernels, on_device(): pl.pallas_call(kernel, out_shape=(jax.ShapeDtypeStruct(lesser.shape, bf16...  170 us
    unnamed x6, local copies, waits for them, and re-layouts  8.22 us
    reshape x2, local copies, waits for them, and re-layouts, on_device(): solved.reshape(count, GROUPS, SIDE, 2, LANES).transpose(0, 2, 3, 1, 4)  4.01 us

profile of v1, /device:TPU:21, one launch (start us, length us, event | category | flops | bytes accessed | tf_op | source)
XLA Modules:
  0.0 186.1 jit_solution(11365091002774346460)
XLA Ops:
  0.6 0.8 copy.10
  1.4 0.6 reshape.19.triples
  2.0 3.6 %copy.11 = bf16[2,384,2,384]{1,3,2,0:T(8,128)(2,1)S(1)} copy(bf16[2,384,2,384]{3,2,1,0:T(2,128)(2,1)} %param.9) | data formatting | bytes 2359296 | tf_op args[4]
  5.6 1.2 copy.12
  6.9 1.6 reshape.21.right
  8.5 169.7 %second_born.1 = (bf16[2,2,384,384]{3,2,1,0:T(8,128)(2,1)}, bf16[2,3,384,256]{3,2,1,0:T(8,128)(2,1)}) custom-call(s32[96]{0:T(128)} %reshape.19.triples, bf16[2,2,384,384]{3,2,1,0:T(8,128)(2,1)} %lesser.1, bf16[2,2,384,384]{3,2,1,0:T(8,128)(2,1)} %greater.1, bf16[2,2,384,384]{3,2,1,0:T(8,128)(2,1)} %diag.1, bf16[2,3,384,256]{3,2,1,0:T(8,128)(2,1)} %reshape.21.right), custom_call_target="tpu_custom_call" | custom-call | tf_op jit(solution)/shard_map/second_born/pallas_call | solution.py:386
  178.2 2.8 %reshape.22 = bf16[2,3,384,2,128]{4,3,2,1,0:T(2,128)(2,1)S(1)} reshape(bf16[2,3,384,256]{3,2,1,0:T(8,128)(2,1)} %get-tuple-element.5) | data formatting | bytes 2359296 | tf_op jit(solution)/shard_map/reshape | solution.py:419
  180.9 1.3 copy.13
  182.2 0.0 copy-start
  182.2 2.8 %copy.14 = bf16[2,384,2,384]{3,2,1,0:T(2,128)(2,1)} copy(bf16[2,384,2,384]{1,3,2,0:T(8,128)(2,1)S(1)} %bitcast.8) | data formatting | bytes 2359296
  185.0 0.0 copy-done
  185.0 1.0 copy.16
Async XLA Ops:
  182.2 2.9 %copy-start = (bf16[2,2,384,384]{3,2,1,0:T(8,128)(2,1)S(1)}, bf16[2,2,384,384]{3,2,1,0:T(8,128)(2,1)}, u32[]{:S(2)}) copy-start(bf16[2,2,384,384]{3,2,1,0:T(8,128)(2,1)} %get-tuple-element.10) | copy-start | bytes 3538948

commit v2 on v1

--- a/solution.py
+++ b/solution.py
@@ -18,8 +18,8 @@
 SUB = 16
 
 
-def expand(tall):
-    real, imag = tall[:, :LANES], tall[:, LANES:]
+def expand(real, imag):
+    tall = jnp.concatenate([real, imag], axis=1)
     turned = jnp.concatenate([-imag, real], axis=1)
     return jnp.concatenate([tall, turned], axis=0)
 
@@ -28,7 +28,7 @@
     triples, lesser, greater, diag, right,
     sigma, solved,
     l0, l1, l2, g0, g1, g2, partner, own_sigma, rows_of, dbuf, rbuf, acc, sol,
-    ex_s, ex_r, loc, zs, zr, ys, yr, ss, sr, rs, rr, dl, ds_, dr, xs, xr, os_, or_, out_s,
+    ex_s, ex_r, ps_s, ps_r, loc, zs, zr, ys, yr, ss, sr, rs, rr, dl, ds_, dr, xs, xr, os_, or_, out_s,
 ):
     lch, gch = (l0, l1, l2), (g0, g1, g2)
     row = lax.axis_index("row")
@@ -57,7 +57,7 @@
         )
 
     barrier = pltpu.get_barrier_semaphore()
-    peers = [pair_dev, sibling, zflip, at(x, 1 - core, y, 1 - zl)]
+    peers = [pair_dev, sibling, zflip, at(x, 1 - core, y, 1 - zl), (row, (1 - zl) * 4 + y, 1 - mom)]
     peers += [y_dev(d) for d in (1, 2, 3)]
     peers += [at((x + d) % 4, core, y, zl) for d in (1, 2, 3)]
     for peer in peers:
@@ -65,8 +65,18 @@
     pl.semaphore_wait(barrier, len(peers))
 
     needed = col < row
-    early = jnp.logical_or(needed, x == 3)
+    last = x == 3
+    ring = y < 2 * x + 1
+    early = jnp.logical_or(needed, last)
     late = jnp.logical_not(early)
+    source = jnp.logical_and(y < row, jnp.logical_not(last))
+    split = jnp.logical_and(source, zl == 0)
+    relay = jnp.logical_and(source, zl == 1)
+    straight = jnp.logical_not(split)
+    begin_now = jnp.logical_and(late, jnp.logical_not(ring))
+    begin_mid = late & relay & ((x != 2) | (y != 0))
+    begin_end = late & ring & jnp.logical_not(begin_mid)
+    pass_dev = (row, (1 - zl) * 4 + y, 1 - mom)
 
     def part(i):
         return pl.ds(i * PART, PART)
@@ -85,25 +95,52 @@
             pltpu.make_async_copy(greater.at[:, :, :, part(i)], gch[i].at[mine], loc.at[i, 1]),
         )
 
+    def right_self(m):
+        return jnp.logical_and(core == zl, zl == m)
+
+    def right_send(m):
+        return remote(right.at[m], rbuf.at[core], rs.at[m], rr.at[core], at(x, zl, y, m))
+
+    def right_keep(m):
+        return pltpu.make_async_copy(right.at[m], rbuf.at[core], rr.at[core])
+
+    def share_right():
+        for m in range(2):
+            pl.when(right_self(m))(lambda m=m: right_keep(m).start())
+            pl.when(jnp.logical_not(right_self(m)))(lambda m=m: right_send(m).start())
+
     def start_exchange():
         for i in range(CHUNKS):
             for copy in exchange(i):
                 copy.start()
 
-    pl.when(early)(start_exchange)
-
-    def right_self(m):
-        return jnp.logical_and(core == zl, zl == m)
-
-    def right_send(m):
-        return remote(right.at[m], rbuf.at[core], rs.at[m], rr.at[core], at(x, zl, y, m))
-
-    def right_keep(m):
-        return pltpu.make_async_copy(right.at[m], rbuf.at[core], rr.at[core])
-
-    for m in range(2):
-        pl.when(right_self(m))(lambda m=m: right_keep(m).start())
-        pl.when(jnp.logical_not(right_self(m)))(lambda m=m: right_send(m).start())
+    theirs = pl.ds(2 * (1 - mom), 2)
+
+    def pass_out(i):
+        return remote(
+            greater.at[:, :, :, part(i)], gch[i].at[theirs], ex_s.at[i, 1], ps_r.at[i], pass_dev
+        )
+
+    def pass_on(i):
+        return remote(gch[i].at[mine], gch[i].at[theirs], ps_s.at[i], ex_r.at[i, 1], zflip)
+
+    def start_lesser(i):
+        exchange(i)[0].start()
+
+    def start_greater(i):
+        pl.when(split)(lambda: pass_out(i).start())
+        pl.when(straight)(lambda: exchange(i)[1].start())
+
+    pl.when(x == 0)(share_right)
+
+    @pl.when(early)
+    def _():
+        for i in (0, 1):
+            start_lesser(i)
+            start_greater(i)
+        pl.when(split)(lambda: pass_out(2).start())
+
+    pl.when(begin_now)(start_exchange)
 
     def diag_keep(q):
         return pltpu.make_async_copy(diag.at[zl, q], dbuf.at[core, :, pl.ds(q * SIDE, SIDE)], dl.at[q])
@@ -117,8 +154,8 @@
         diag_keep(q).start()
         diag_send(q).start()
     for i in range(CHUNKS):
-        for copy in keep(i):
-            copy.start()
+        keep(i)[0].start()
+        pl.when(jnp.logical_not(relay))(lambda i=i: keep(i)[1].start())
 
     def sigma_out(i, q):
         return pltpu.make_async_copy(
@@ -147,8 +184,7 @@
                 sum_real = jnp.zeros((SUB, SIDE), jnp.float32)
                 sum_imag = jnp.zeros((SUB, SIDE), jnp.float32)
                 for p in range(PAIRS):
-                    base = (2 * mom + m) * (3 * PAIRS) + 3 * p
-                    a, b, c = triples[base], triples[base + 1], triples[base + 2]
+                    a, b, c = (triples[n, 2 * mom + m, p] for n in range(3))
                     ar = lch[i][a, 0, here, :].astype(jnp.float32)
                     ai = lch[i][a, 1, here, :].astype(jnp.float32)
                     br = lch[i][b, 0, here, :].astype(jnp.float32)
@@ -215,9 +251,139 @@
                     remote(tile, tile, ss.at[j, i], yr.at[j, i], sibling).wait_recv()
                     side_send(j, i).start()
 
+    for q in range(2):
+        diag_keep(q).wait()
+        dst = dbuf.at[1 - core, :, pl.ds(q * SIDE, SIDE)]
+        remote(diag.at[zl, q], dst, ds_.at[q], dr.at[q], sibling).wait_recv()
+    def take_right():
+        for q in range(2):
+            from_self = jnp.logical_and(core == q, zl == core)
+
+            @pl.when(from_self)
+            def _(q=q):
+                pltpu.make_async_copy(right.at[0], rbuf.at[q], rr.at[q]).wait()
+
+            @pl.when(jnp.logical_not(from_self))
+            def _(q=q):
+                remote(right.at[0], rbuf.at[q], rs.at[0], rr.at[q], sibling).wait_recv()
+
+    def sol_send(q, g, d):
+        tile = sol.at[2 * x + q, g]
+        return remote(tile, tile, xs.at[q, g, d - 1], xr.at[2 * x + q, g], x_dev(d))
+
+    def out_self(q):
+        return jnp.logical_and(core == q, zl == core)
+
+    def out_tile(m, g):
+        start = g * LANES if isinstance(g, int) else pl.multiple_of(g * LANES, LANES)
+        return solved.at[m, :, :, pl.ds(start, LANES)]
+
+    def out_send(q, g):
+        return remote(
+            sol.at[2 * x + q, g], out_tile(zl, g), os_.at[q, g], or_.at[zl, g], at(x, q, y, core)
+        )
+
+    def out_keep(q, g):
+        return pltpu.make_async_copy(sol.at[2 * x + q, g], out_tile(zl, g), or_.at[zl, g])
+
+    def side_wait(j, which):
+        @pl.when(core != which)
+        def _():
+            for i in range(CHUNKS):
+                side_in(j, i).wait_recv()
+
+    def add_right(q, g):
+        lanes = pl.ds(pl.multiple_of(g * LANES, LANES), LANES)
+        for c in range(2):
+            acc[g, q, :, c * LANES : (c + 1) * LANES] += rbuf[q, c, :, lanes].astype(jnp.float32)
+
+    def solve(q, g):
+        pending = acc[g, q].astype(jnp.bfloat16)
+        answer = jnp.dot(
+            dbuf[q], expand(pending[:, :LANES], pending[:, LANES:]), preferred_element_type=jnp.float32
+        ).astype(jnp.bfloat16)
+        sol[2 * x + q, g, 0] = answer[:, :LANES]
+        sol[2 * x + q, g, 1] = answer[:, LANES:]
+        pl.when(x < 3)(lambda: sol_send(q, g, 1).start())
+        pl.when(x == 0)(lambda: sol_send(q, g, 3).start())
+        pl.when(x == 1)(lambda: sol_send(q, g, 2).start())
+        pl.when(out_self(q))(lambda: out_keep(q, g).start())
+        pl.when(jnp.logical_not(out_self(q)))(lambda: out_send(q, g).start())
+
+    def far_sends(q):
+        @pl.when(x == 0)
+        def _():
+            for g in range(GROUPS):
+                sol_send(q, g, 2).start()
+
+    def first(g, carry):
+        acc[g] = jnp.zeros(acc.shape[1:], jnp.float32)
+
+        def update(step, c):
+            for t in range(2):
+                j = 2 * step + t
+                tile = sol.at[j, g]
+                remote(tile, tile, xs.at[0, g, 0], xr.at[j, g], sibling).wait_recv()
+
+                @pl.when(g == 0)
+                def _(j=j):
+                    side_wait(j, 0)
+                    side_wait(j, 1)
+
+                factor = expand(sol[j, g, 0], sol[j, g, 1])
+                for q in range(2):
+                    acc[g, q] += weight * jnp.dot(
+                        rows_of[q, j], factor, preferred_element_type=jnp.float32
+                    )
+            return c
+
+        lax.fori_loop(0, x, update, 0)
+        pl.when((g == 0) & (x > 0))(take_right)
+        for q in range(2):
+            add_right(q, g)
+        solve(0, g)
+        return carry
+
+    def second(g, carry):
+        @pl.when(g == 0)
+        def _():
+            side_wait(2 * x, 1)
+
+        acc[g, 1] += weight * jnp.dot(
+            rows_of[1, 2 * x], expand(sol[2 * x, g, 0], sol[2 * x, g, 1]), preferred_element_type=jnp.float32
+        )
+        solve(1, g)
+        return carry
+
+    @pl.when(x == 0)
+    def _():
+        take_right()
+        lax.fori_loop(0, GROUPS, first, 0)
+        far_sends(0)
+
+    def relay_step(i):
+        @pl.when(relay)
+        def _():
+            remote(gch[i].at[mine], gch[i].at[mine], ps_s.at[i], ps_r.at[i], zflip).wait_recv()
+            pass_on(i).start()
+
+    relay_step(0)
     for i in range(CHUNKS):
+        if i + 1 < CHUNKS:
+            relay_step(i + 1)
+        if i == 1:
+            @pl.when(begin_mid)
+            def _():
+                pl.when(x > 0)(share_right)
+                start_exchange()
+
         @pl.when(early)
         def _(i=i):
+            @pl.when(relay)
+            def _():
+                pass_on(i).wait_send()
+                keep(i)[1].start()
+
             compute_sigma(i)
 
         @pl.when(needed)
@@ -227,6 +393,13 @@
                 y_send(0, i, d).start()
             side_own(i).start()
 
+        if i == 0:
+            pl.when(early)(lambda: start_lesser(2))
+        elif i == 1:
+            pl.when(early & straight)(lambda: start_greater(2))
+        else:
+            pl.when((x > 0) & jnp.logical_not(begin_mid))(share_right)
+
         @pl.when(other_needed)
         def _(i=i):
             hop_in(i).wait_recv()
@@ -237,99 +410,34 @@
         if i:
             gathered(i - 1)
     gathered(CHUNKS - 1)
-    pl.when(late)(start_exchange)
-
-    for q in range(2):
-        diag_keep(q).wait()
-        dst = dbuf.at[1 - core, :, pl.ds(q * SIDE, SIDE)]
-        remote(diag.at[zl, q], dst, ds_.at[q], dr.at[q], sibling).wait_recv()
-    for q in range(2):
-        from_self = jnp.logical_and(core == q, zl == core)
-
-        @pl.when(from_self)
-        def _(q=q):
-            pltpu.make_async_copy(right.at[0], rbuf.at[q], rr.at[q]).wait()
-
-        @pl.when(jnp.logical_not(from_self))
-        def _(q=q):
-            remote(right.at[0], rbuf.at[q], rs.at[0], rr.at[q], sibling).wait_recv()
-
-    def sol_send(q, g, d):
-        tile = sol.at[2 * x + q, g]
-        return remote(tile, tile, xs.at[q, g, d - 1], xr.at[2 * x + q, g], x_dev(d))
-
-    def out_self(q):
-        return jnp.logical_and(core == q, zl == core)
-
-    def out_send(q, g):
-        return remote(
-            sol.at[2 * x + q, g], solved.at[zl, g], os_.at[q, g], or_.at[zl, g], at(x, q, y, core)
-        )
-
-    def out_keep(q, g):
-        return pltpu.make_async_copy(sol.at[2 * x + q, g], solved.at[zl, g], or_.at[zl, g])
-
-    def side_wait(j, which):
-        @pl.when(core != which)
+    pl.when(begin_end & (x > 0))(start_exchange)
+
+    def both(g, carry):
+        @pl.when(x > 0)
+        def _():
+            first(g, 0)
+
+        return second(g, carry)
+
+    lax.fori_loop(0, GROUPS, both, 0)
+    far_sends(1)
+    pl.when(begin_end & (x == 0))(start_exchange)
+
+    @pl.when(late)
+    def _():
+        @pl.when(relay)
         def _():
             for i in range(CHUNKS):
-                side_in(j, i).wait_recv()
-
-    def group(g, carry):
-        for q in range(2):
-            acc[q] = rbuf[q, g].astype(jnp.float32)
-
-        def update(step, c):
-            for t in range(2):
-                j = 2 * step + t
-                tile = sol.at[j, g]
-                remote(tile, tile, xs.at[0, g, 0], xr.at[j, g], sibling).wait_recv()
-
-                @pl.when(g == 0)
-                def _(j=j):
-                    side_wait(j, 0)
-                    side_wait(j, 1)
-
-                factor = expand(sol[j, g])
-                for q in range(2):
-                    acc[q] += weight * jnp.dot(
-                        rows_of[q, j], factor, preferred_element_type=jnp.float32
-                    )
-            return c
-
-        lax.fori_loop(0, x, update, 0)
-
-        for q in range(2):
-            answer = jnp.dot(
-                dbuf[q], expand(acc[q].astype(jnp.bfloat16)), preferred_element_type=jnp.float32
-            ).astype(jnp.bfloat16)
-            sol[2 * x + q, g] = answer
-            for d in (1, 2, 3):
-                @pl.when(x + d < 4)
-                def _(q=q, d=d):
-                    sol_send(q, g, d).start()
-            pl.when(out_self(q))(lambda q=q: out_keep(q, g).start())
-            pl.when(jnp.logical_not(out_self(q)))(lambda q=q: out_send(q, g).start())
-            if q == 0:
-                @pl.when(g == 0)
-                def _():
-                    side_wait(2 * x, 1)
-
-                acc[1] += weight * jnp.dot(
-                    rows_of[1, 2 * x], expand(answer), preferred_element_type=jnp.float32
-                )
-        return carry
-
-    lax.fori_loop(0, GROUPS, group, 0)
-
-    @pl.when(late)
-    def _():
+                pass_on(i).wait_send()
+                keep(i)[1].start()
+
         for i in range(CHUNKS):
             compute_sigma(i)
 
     for i in range(CHUNKS):
-        for copy in exchange(i):
-            copy.wait_send()
+        exchange(i)[0].wait_send()
+        pl.when(split)(lambda i=i: pass_out(i).wait_send())
+        pl.when(straight)(lambda i=i: exchange(i)[1].wait_send())
         for q in range(2):
             sigma_out(i, q).wait()
 
@@ -369,17 +477,15 @@
 
             @pl.when(from_self)
             def _(m=m, g=g):
-                pltpu.make_async_copy(sol.at[0, g], solved.at[m, g], or_.at[m, g]).wait()
+                pltpu.make_async_copy(sol.at[0, g], out_tile(m, g), or_.at[m, g]).wait()
 
             @pl.when(jnp.logical_not(from_self))
             def _(m=m, g=g):
-                remote(sol.at[0, g], solved.at[m, g], os_.at[0, g], or_.at[m, g], sibling).wait_recv()
+                remote(sol.at[0, g], out_tile(m, g), os_.at[0, g], or_.at[m, g], sibling).wait_recv()
 
 
 def on_device(lesser, greater, triples, diag_inverse, right_side):
-    count = right_side.shape[0]
-    right = right_side.reshape(count, SIDE, 2, GROUPS, LANES).transpose(0, 3, 1, 2, 4)
-    right = right.reshape(count, GROUPS, SIDE, 2 * LANES)
+    right = right_side.transpose(0, 2, 1, 3)
     bf16, f32 = jnp.bfloat16, jnp.float32
     dma = pltpu.SemaphoreType.DMA
     hbm = pl.BlockSpec(memory_space=pl.ANY)
@@ -398,10 +504,10 @@
             pltpu.VMEM((2, SIDE, WIDE), bf16),
             pltpu.VMEM((2, 8, SIDE, WIDE), bf16),
             pltpu.VMEM((2, SIDE, WIDE), bf16),
-            pltpu.VMEM((2, GROUPS, SIDE, 2 * LANES), bf16),
-            pltpu.VMEM((2, SIDE, 2 * LANES), f32),
-            pltpu.VMEM((8, GROUPS, SIDE, 2 * LANES), bf16),
-            dma((CHUNKS, 2)), dma((CHUNKS, 2)), dma((CHUNKS, 2)),
+            pltpu.VMEM((2, 2, SIDE, SIDE), bf16),
+            pltpu.VMEM((GROUPS, 2, SIDE, 2 * LANES), f32),
+            pltpu.VMEM((8, GROUPS, 2, SIDE, LANES), bf16),
+            dma((CHUNKS, 2)), dma((CHUNKS, 2)), dma((CHUNKS,)), dma((CHUNKS,)), dma((CHUNKS, 2)),
             dma((CHUNKS,)), dma((CHUNKS,)),
             dma((2, CHUNKS, 3)), dma((8, CHUNKS)),
             dma((8, CHUNKS)), dma((8, CHUNKS)),
@@ -415,9 +521,8 @@
             collective_id=0, has_side_effects=True, vmem_limit_bytes=56 * 1024 * 1024
         ),
         name="second_born",
-    )(triples.reshape(-1), lesser, greater, diag_inverse, right)
-    solved = solved.reshape(count, GROUPS, SIDE, 2, LANES).transpose(0, 2, 3, 1, 4)
-    return (sigma, solved.reshape(right_side.shape))
+    )(triples.transpose(2, 0, 1), lesser, greater, diag_inverse, right)
+    return (sigma, solved.transpose(0, 2, 1, 3))
 
 
 def solution(mesh):

time: 186 us -> 138 us (0.74)
  the two profiles are of different devices: /device:TPU:21 before, /device:TPU:23 now
where the time goes in v2:
time: 138 us
  Pallas kernels  130 us (94%)
  local copies, waits for them, and re-layouts  7.04 us (5%)
    pallas_call x1, Pallas kernels, on_device(): pl.pallas_call(kernel, out_shape=(jax.ShapeDtypeStruct(lesser.shape, bf16...  130 us
    unnamed x5, local copies, waits for them, and re-layouts  7.04 us

profile of v2, /device:TPU:23, one launch (start us, length us, event | category | flops | bytes accessed | tf_op | source)
XLA Modules:
  0.0 138.0 jit_solution(9082039803604742662)
XLA Ops:
  0.6 2.4 %copy.10 = bf16[2,384,2,384]{3,1,2,0:T(8,128)(2,1)} copy(bf16[2,384,2,384]{3,2,1,0:T(2,128)(2,1)} %param.9) | data formatting | bytes 2359296 | tf_op args[4]
  3.1 130.4 %second_born.1 = (bf16[2,2,384,384]{3,2,1,0:T(8,128)(2,1)}, bf16[2,2,384,384]{3,2,1,0:T(8,128)(2,1)}) custom-call(s32[3,4,8]{2,1,0:T(4,128)} %bitcast.7, bf16[2,2,384,384]{3,2,1,0:T(8,128)(2,1)} %lesser.1, bf16[2,2,384,384]{3,2,1,0:T(8,128)(2,1)} %greater.1, bf16[2,2,384,384]{3,2,1,0:T(8,128)(2,1)} %diag.1, bf16[2,2,384,384]{3,2,1,0:T(8,128)(2,1)} %bitcast.5), custom_call_target="tpu_custom_call" | custom-call | tf_op jit(solution)/shard_map/second_born/pallas_call | solution.py:492
  133.4 0.0 copy-start
  133.4 3.6 %copy.8 = bf16[2,384,2,384]{3,2,1,0:T(2,128)(2,1)} copy(bf16[2,384,2,384]{3,1,2,0:T(8,128)(2,1)} %bitcast.6) | data formatting | bytes 2359296
  137.0 0.0 copy-done
  137.0 1.0 copy.12
Async XLA Ops:
  133.4 3.6 %copy-start = (bf16[2,2,384,384]{3,2,1,0:T(8,128)(2,1)S(1)}, bf16[2,2,384,384]{3,2,1,0:T(8,128)(2,1)}, u32[]{:S(2)}) copy-start(bf16[2,2,384,384]{3,2,1,0:T(8,128)(2,1)} %get-tuple-element.10) | copy-start | bytes 3538948

commit v3 on v2

--- a/solution.py
+++ b/solution.py
@@ -27,7 +27,7 @@
 def kernel(
     triples, lesser, greater, diag, right,
     sigma, solved,
-    l0, l1, l2, g0, g1, g2, partner, own_sigma, rows_of, dbuf, rbuf, acc, sol,
+    l0, l1, l2, g0, g1, g2, partner, own_sigma, rows_of, dbuf, rbuf, acc, sol, obuf,
     ex_s, ex_r, ps_s, ps_r, loc, zs, zr, ys, yr, ss, sr, rs, rr, dl, ds_, dr, xs, xr, os_, or_, out_s,
 ):
     lch, gch = (l0, l1, l2), (g0, g1, g2)
@@ -69,7 +69,7 @@
     ring = y < 2 * x + 1
     early = jnp.logical_or(needed, last)
     late = jnp.logical_not(early)
-    source = jnp.logical_and(y < row, jnp.logical_not(last))
+    source = (y < row) & jnp.logical_not(last) & ((row != 5) | (y != 0))
     split = jnp.logical_and(source, zl == 0)
     relay = jnp.logical_and(source, zl == 1)
     straight = jnp.logical_not(split)
@@ -131,15 +131,15 @@
         pl.when(split)(lambda: pass_out(i).start())
         pl.when(straight)(lambda: exchange(i)[1].start())
 
-    pl.when(x == 0)(share_right)
-
     @pl.when(early)
     def _():
         for i in (0, 1):
             start_lesser(i)
             start_greater(i)
         pl.when(split)(lambda: pass_out(2).start())
-
+        pl.when(x == 0)(lambda: start_lesser(2))
+
+    pl.when(x == 0)(share_right)
     pl.when(begin_now)(start_exchange)
 
     def diag_keep(q):
@@ -280,11 +280,11 @@
 
     def out_send(q, g):
         return remote(
-            sol.at[2 * x + q, g], out_tile(zl, g), os_.at[q, g], or_.at[zl, g], at(x, q, y, core)
+            obuf.at[q, g], out_tile(zl, g), os_.at[q, g], or_.at[zl, g], at(x, q, y, core)
         )
 
     def out_keep(q, g):
-        return pltpu.make_async_copy(sol.at[2 * x + q, g], out_tile(zl, g), or_.at[zl, g])
+        return pltpu.make_async_copy(obuf.at[q, g], out_tile(zl, g), or_.at[zl, g])
 
     def side_wait(j, which):
         @pl.when(core != which)
@@ -295,26 +295,32 @@
     def add_right(q, g):
         lanes = pl.ds(pl.multiple_of(g * LANES, LANES), LANES)
         for c in range(2):
-            acc[g, q, :, c * LANES : (c + 1) * LANES] += rbuf[q, c, :, lanes].astype(jnp.float32)
+            acc[g, q, :, c * LANES : (c + 1) * LANES] += rbuf[q, :, c, lanes].astype(jnp.float32)
 
     def solve(q, g):
         pending = acc[g, q].astype(jnp.bfloat16)
         answer = jnp.dot(
             dbuf[q], expand(pending[:, :LANES], pending[:, LANES:]), preferred_element_type=jnp.float32
         ).astype(jnp.bfloat16)
-        sol[2 * x + q, g, 0] = answer[:, :LANES]
-        sol[2 * x + q, g, 1] = answer[:, LANES:]
+        real, imag = answer[:, :LANES], answer[:, LANES:]
+        sol[2 * x + q, g, 0] = real
+        sol[2 * x + q, g, 1] = imag
         pl.when(x < 3)(lambda: sol_send(q, g, 1).start())
         pl.when(x == 0)(lambda: sol_send(q, g, 3).start())
-        pl.when(x == 1)(lambda: sol_send(q, g, 2).start())
+        obuf[q, g] = jnp.stack([real, imag], axis=1)
         pl.when(out_self(q))(lambda: out_keep(q, g).start())
         pl.when(jnp.logical_not(out_self(q)))(lambda: out_send(q, g).start())
 
-    def far_sends(q):
-        @pl.when(x == 0)
+    def row_on(j, g):
+        tile = sol.at[j, g]
+        return remote(tile, tile, xs.at[j, g, 0], xr.at[j, g], x_dev(-1))
+
+    def relay_row(j):
+        @pl.when(last)
         def _():
             for g in range(GROUPS):
-                sol_send(q, g, 2).start()
+                row_on(j, g).wait_recv()
+                row_on(j, g).start()
 
     def first(g, carry):
         acc[g] = jnp.zeros(acc.shape[1:], jnp.float32)
@@ -323,7 +329,10 @@
             for t in range(2):
                 j = 2 * step + t
                 tile = sol.at[j, g]
-                remote(tile, tile, xs.at[0, g, 0], xr.at[j, g], sibling).wait_recv()
+
+                @pl.when(jnp.logical_not(last) | (j > 1))
+                def _(tile=tile, j=j):
+                    remote(tile, tile, xs.at[0, g, 0], xr.at[j, g], sibling).wait_recv()
 
                 @pl.when(g == 0)
                 def _(j=j):
@@ -359,7 +368,6 @@
     def _():
         take_right()
         lax.fori_loop(0, GROUPS, first, 0)
-        far_sends(0)
 
     def relay_step(i):
         @pl.when(relay)
@@ -371,6 +379,8 @@
     for i in range(CHUNKS):
         if i + 1 < CHUNKS:
             relay_step(i + 1)
+        if i:
+            relay_row(i - 1)
         if i == 1:
             @pl.when(begin_mid)
             def _():
@@ -394,7 +404,7 @@
             side_own(i).start()
 
         if i == 0:
-            pl.when(early)(lambda: start_lesser(2))
+            pl.when(early & (x > 0))(lambda: start_lesser(2))
         elif i == 1:
             pl.when(early & straight)(lambda: start_greater(2))
         else:
@@ -420,7 +430,13 @@
         return second(g, carry)
 
     lax.fori_loop(0, GROUPS, both, 0)
-    far_sends(1)
+
+    @pl.when(x == 1)
+    def _():
+        for g in range(GROUPS):
+            for q in range(2):
+                sol_send(q, g, 2).start()
+
     pl.when(begin_end & (x == 0))(start_exchange)
 
     @pl.when(late)
@@ -467,25 +483,24 @@
         diag_send(q).wait_send()
     for g in range(GROUPS):
         for q in range(2):
-            for d in (1, 2, 3):
-                @pl.when(x + d < 4)
-                def _(q=q, g=g, d=d):
-                    sol_send(q, g, d).wait_send()
+            pl.when(x < 3)(lambda q=q, g=g: sol_send(q, g, 1).wait_send())
+            pl.when(x == 1)(lambda q=q, g=g: sol_send(q, g, 2).wait_send())
+            pl.when(x == 0)(lambda q=q, g=g: sol_send(q, g, 3).wait_send())
+            pl.when(last)(lambda q=q, g=g: row_on(q, g).wait_send())
             pl.when(jnp.logical_not(out_self(q)))(lambda q=q, g=g: out_send(q, g).wait_send())
         for m in range(2):
             from_self = jnp.logical_and(core == zl, zl == m)
 
             @pl.when(from_self)
             def _(m=m, g=g):
-                pltpu.make_async_copy(sol.at[0, g], out_tile(m, g), or_.at[m, g]).wait()
+                pltpu.make_async_copy(obuf.at[0, g], out_tile(m, g), or_.at[m, g]).wait()
 
             @pl.when(jnp.logical_not(from_self))
             def _(m=m, g=g):
-                remote(sol.at[0, g], out_tile(m, g), os_.at[0, g], or_.at[m, g], sibling).wait_recv()
+                remote(obuf.at[0, g], out_tile(m, g), os_.at[0, g], or_.at[m, g], sibling).wait_recv()
 
 
 def on_device(lesser, greater, triples, diag_inverse, right_side):
-    right = right_side.transpose(0, 2, 1, 3)
     bf16, f32 = jnp.bfloat16, jnp.float32
     dma = pltpu.SemaphoreType.DMA
     hbm = pl.BlockSpec(memory_space=pl.ANY)
@@ -493,7 +508,7 @@
         kernel,
         out_shape=(
             jax.ShapeDtypeStruct(lesser.shape, bf16),
-            jax.ShapeDtypeStruct(right.shape, bf16),
+            jax.ShapeDtypeStruct(right_side.shape, bf16),
         ),
         in_specs=[pl.BlockSpec(memory_space=pltpu.SMEM), hbm, hbm, hbm, hbm],
         out_specs=(hbm, hbm),
@@ -504,9 +519,10 @@
             pltpu.VMEM((2, SIDE, WIDE), bf16),
             pltpu.VMEM((2, 8, SIDE, WIDE), bf16),
             pltpu.VMEM((2, SIDE, WIDE), bf16),
-            pltpu.VMEM((2, 2, SIDE, SIDE), bf16),
+            pltpu.VMEM((2, SIDE, 2, SIDE), bf16),
             pltpu.VMEM((GROUPS, 2, SIDE, 2 * LANES), f32),
             pltpu.VMEM((8, GROUPS, 2, SIDE, LANES), bf16),
+            pltpu.VMEM((2, GROUPS, SIDE, 2, LANES), bf16),
             dma((CHUNKS, 2)), dma((CHUNKS, 2)), dma((CHUNKS,)), dma((CHUNKS,)), dma((CHUNKS, 2)),
             dma((CHUNKS,)), dma((CHUNKS,)),
             dma((2, CHUNKS, 3)), dma((8, CHUNKS)),
@@ -521,8 +537,8 @@
             collective_id=0, has_side_effects=True, vmem_limit_bytes=56 * 1024 * 1024
         ),
         name="second_born",
-    )(triples.transpose(2, 0, 1), lesser, greater, diag_inverse, right)
-    return (sigma, solved.transpose(0, 2, 1, 3))
+    )(triples.transpose(2, 0, 1), lesser, greater, diag_inverse, right_side)
+    return (sigma, solved)
 
 
 def solution(mesh):

time: 138 us -> 124 us (0.90); the launches traced: 138 us -> 122 us
  Pallas kernels: 130 us -> 118 us
  local copies, waits for them, and re-layouts: 7.04 us -> 3.51 us
    pallas_call x1, Pallas kernels: 130 us -> 118 us  [on_device(): pl.pallas_call(kernel, out_shape=(jax.ShapeDtypeStruct(lesser.shape, bf16...]
    unnamed x5 -> x4, local copies, waits for them, and re-layouts: 7.04 us -> 3.51 us
where the time goes in v3:
time: 124 us; the launch traced here: 122 us
  Pallas kernels  118 us (95%)
  local copies, waits for them, and re-layouts  3.51 us (3%)
    pallas_call x1, Pallas kernels, on_device(): pl.pallas_call(kernel, out_shape=(jax.ShapeDtypeStruct(lesser.shape, bf16...  118 us
    unnamed x4, local copies, waits for them, and re-layouts  3.51 us

profile of v3, /device:TPU:23, one launch (start us, length us, event | category | flops | bytes accessed | tf_op | source)
XLA Modules:
  0.0 121.7 jit_solution(13310026374962165243)
XLA Ops:
  0.6 117.5 %second_born.1 = (bf16[2,2,384,384]{3,2,1,0:T(8,128)(2,1)}, bf16[2,384,2,384]{3,2,1,0:T(2,128)(2,1)}) custom-call(s32[3,4,8]{2,1,0:T(4,128)} %bitcast.1, bf16[2,2,384,384]{3,2,1,0:T(8,128)(2,1)} %lesser.1, bf16[2,2,384,384]{3,2,1,0:T(8,128)(2,1)} %greater.1, bf16[2,2,384,384]{3,2,1,0:T(8,128)(2,1)} %diag.1, bf16[2,384,2,384]{3,2,1,0:T(2,128)(2,1)} %right.1), custom_call_target="tpu_custom_call" | custom-call | tf_op jit(solution)/shard_map/second_born/pallas_call | solution.py:507
  118.2 0.0 copy-start
  118.2 2.5 %copy.9 = bf16[2,2,384,384]{3,2,1,0:T(8,128)(2,1)} copy(bf16[2,2,384,384]{3,2,1,0:T(8,128)(2,1)} %get-tuple-element.4) | data formatting | bytes 2359296
  120.7 0.0 copy-done
  120.7 1.0 copy.10
Async XLA Ops:
  118.2 2.5 %copy-start = (bf16[2,384,2,384]{3,2,1,0:T(2,128)(2,1)S(1)}, bf16[2,384,2,384]{3,2,1,0:T(2,128)(2,1)}, u32[]{:S(2)}) copy-start(bf16[2,384,2,384]{3,2,1,0:T(2,128)(2,1)} %get-tuple-element.5) | copy-start | bytes 3538948

commit v4 on v3

--- a/solution.py
+++ b/solution.py
@@ -27,8 +27,8 @@
 def kernel(
     triples, lesser, greater, diag, right,
     sigma, solved,
-    l0, l1, l2, g0, g1, g2, partner, own_sigma, rows_of, dbuf, rbuf, acc, sol, obuf,
-    ex_s, ex_r, ps_s, ps_r, loc, zs, zr, ys, yr, ss, sr, rs, rr, dl, ds_, dr, xs, xr, os_, or_, out_s,
+    l0, l1, l2, g0, g1, g2, partner, own_sigma, rows_of, dbuf, rbuf, acc, sol, obuf, raw, plan,
+    ex_s, ex_r, ps_s, ps_r, loc, zs, zr, ys, yr, ss, sr, rs, rr, dl, ds_, dr, xs, xr, os_, or_, out_s, raw_s,
 ):
     lch, gch = (l0, l1, l2), (g0, g1, g2)
     row = lax.axis_index("row")
@@ -76,6 +76,7 @@
     begin_now = jnp.logical_and(late, jnp.logical_not(ring))
     begin_mid = late & relay & ((x != 2) | (y != 0))
     begin_end = late & ring & jnp.logical_not(begin_mid)
+    three = ((x == 2) & (y == 0)) | ((x == 1) & (core == 0))
     pass_dev = (row, (1 - zl) * 4 + y, 1 - mom)
 
     def part(i):
@@ -98,16 +99,33 @@
     def right_self(m):
         return jnp.logical_and(core == zl, zl == m)
 
-    def right_send(m):
-        return remote(right.at[m], rbuf.at[core], rs.at[m], rr.at[core], at(x, zl, y, m))
-
-    def right_keep(m):
-        return pltpu.make_async_copy(right.at[m], rbuf.at[core], rr.at[core])
+    def right_send(m, g):
+        return remote(plan.at[m, g], rbuf.at[core, g], rs.at[m, g], rr.at[core, g], at(x, zl, y, m))
+
+    def right_keep(m, g):
+        return pltpu.make_async_copy(plan.at[m, g], rbuf.at[core, g], rr.at[core, g])
 
     def share_right():
-        for m in range(2):
-            pl.when(right_self(m))(lambda m=m: right_keep(m).start())
-            pl.when(jnp.logical_not(right_self(m)))(lambda m=m: right_send(m).start())
+        for g in range(GROUPS):
+            for m in range(2):
+                pl.when(right_self(m))(lambda m=m: right_keep(m, g).start())
+                pl.when(jnp.logical_not(right_self(m)))(lambda m=m: right_send(m, g).start())
+
+    raw_in = pltpu.make_async_copy(right, raw, raw_s.at[0])
+    raw_in.start()
+
+    def turn_right():
+        raw_in.wait()
+
+        def turn_group(t, carry):
+            m, g = t // GROUPS, t % GROUPS
+            lanes = pl.ds(pl.multiple_of(g * LANES, LANES), LANES)
+            both_parts = raw[m, :, :, lanes].astype(jnp.float32)
+            for c in range(2):
+                plan[m, g, :, c * LANES : (c + 1) * LANES] = both_parts[:, c, :].astype(jnp.bfloat16)
+            return carry
+
+        lax.fori_loop(0, 2 * GROUPS, turn_group, 0)
 
     def start_exchange():
         for i in range(CHUNKS):
@@ -127,18 +145,29 @@
     def start_lesser(i):
         exchange(i)[0].start()
 
+    RELAYED = 2
+
     def start_greater(i):
-        pl.when(split)(lambda: pass_out(i).start())
-        pl.when(straight)(lambda: exchange(i)[1].start())
+        if i < RELAYED:
+            pl.when(split)(lambda: pass_out(i).start())
+            pl.when(straight)(lambda: exchange(i)[1].start())
+        else:
+            pl.when(jnp.logical_not(split & three))(lambda: exchange(i)[1].start())
 
     @pl.when(early)
     def _():
         for i in (0, 1):
             start_lesser(i)
             start_greater(i)
-        pl.when(split)(lambda: pass_out(2).start())
-        pl.when(x == 0)(lambda: start_lesser(2))
-
+
+        pl.when(split & three)(lambda: pass_out(2).start())
+
+        @pl.when(x == 0)
+        def _():
+            start_lesser(2)
+            start_greater(2)
+
+    turn_right()
     pl.when(x == 0)(share_right)
     pl.when(begin_now)(start_exchange)
 
@@ -155,7 +184,10 @@
         diag_send(q).start()
     for i in range(CHUNKS):
         keep(i)[0].start()
-        pl.when(jnp.logical_not(relay))(lambda i=i: keep(i)[1].start())
+        if i < RELAYED:
+            pl.when(jnp.logical_not(relay))(lambda i=i: keep(i)[1].start())
+        else:
+            pl.when(jnp.logical_not(relay & three))(lambda i=i: keep(i)[1].start())
 
     def sigma_out(i, q):
         return pltpu.make_async_copy(
@@ -177,36 +209,37 @@
 
         lax.fori_loop(0, 4, turn, 0)
 
-        def block(s, carry):
+        def block(m, s, carry):
             here = pl.ds(pl.multiple_of(s * SUB, SUB), SUB)
             there = pl.ds(pl.multiple_of(i * PART + s * SUB, SUB), SUB)
-            for m in range(2):
-                sum_real = jnp.zeros((SUB, SIDE), jnp.float32)
-                sum_imag = jnp.zeros((SUB, SIDE), jnp.float32)
-                for p in range(PAIRS):
-                    a, b, c = (triples[n, 2 * mom + m, p] for n in range(3))
-                    ar = lch[i][a, 0, here, :].astype(jnp.float32)
-                    ai = lch[i][a, 1, here, :].astype(jnp.float32)
-                    br = lch[i][b, 0, here, :].astype(jnp.float32)
-                    bi = lch[i][b, 1, here, :].astype(jnp.float32)
-                    cr = partner[c, 0, here, :].astype(jnp.float32)
-                    ci = partner[c, 1, here, :].astype(jnp.float32)
-                    pr = ar * br - ai * bi
-                    pi = ar * bi + ai * br
-                    sum_real += pr * cr - pi * ci
-                    sum_imag += pr * ci + pi * cr
-                sig_real = (sum_real * (1.0 / PAIRS)).astype(jnp.bfloat16)
-                sig_imag = (sum_imag * (1.0 / PAIRS)).astype(jnp.bfloat16)
-                own_sigma[m, there, 0:SIDE] = sig_real
-                own_sigma[m, there, SIDE:WIDE] = sig_imag
-
-                @pl.when(zl == m)
-                def _():
-                    rows_of[core, col, there, 0:SIDE] = sig_real
-                    rows_of[core, col, there, SIDE:WIDE] = sig_imag
+            sum_real = jnp.zeros((SUB, SIDE), jnp.float32)
+            sum_imag = jnp.zeros((SUB, SIDE), jnp.float32)
+            for p in range(PAIRS):
+                a, b, c = (triples[n, 2 * mom + m, p] for n in range(3))
+                ar = lch[i][a, 0, here, :].astype(jnp.float32)
+                ai = lch[i][a, 1, here, :].astype(jnp.float32)
+                br = lch[i][b, 0, here, :].astype(jnp.float32)
+                bi = lch[i][b, 1, here, :].astype(jnp.float32)
+                cr = partner[c, 0, here, :].astype(jnp.float32)
+                ci = partner[c, 1, here, :].astype(jnp.float32)
+                pr = ar * br - ai * bi
+                pi = ar * bi + ai * br
+                sum_real += pr * cr - pi * ci
+                sum_imag += pr * ci + pi * cr
+            sig_real = (sum_real * (1.0 / PAIRS)).astype(jnp.bfloat16)
+            sig_imag = (sum_imag * (1.0 / PAIRS)).astype(jnp.bfloat16)
+            own_sigma[m, there, 0:SIDE] = sig_real
+            own_sigma[m, there, SIDE:WIDE] = sig_imag
+
+            @pl.when(zl == m)
+            def _():
+                rows_of[core, col, there, 0:SIDE] = sig_real
+                rows_of[core, col, there, SIDE:WIDE] = sig_imag
             return carry
 
-        lax.fori_loop(0, PART // SUB, block, 0)
+        lax.fori_loop(0, PART // SUB, lambda s, c: block(1 - zl, s, c), 0)
+        pl.when(needed)(lambda: hop(i).start())
+        lax.fori_loop(0, PART // SUB, lambda s, c: block(zl, s, c), 0)
         for q in range(2):
             sigma_out(i, q).start()
 
@@ -255,17 +288,17 @@
         diag_keep(q).wait()
         dst = dbuf.at[1 - core, :, pl.ds(q * SIDE, SIDE)]
         remote(diag.at[zl, q], dst, ds_.at[q], dr.at[q], sibling).wait_recv()
-    def take_right():
+    def take_right(g):
         for q in range(2):
             from_self = jnp.logical_and(core == q, zl == core)
 
             @pl.when(from_self)
             def _(q=q):
-                pltpu.make_async_copy(right.at[0], rbuf.at[q], rr.at[q]).wait()
+                pltpu.make_async_copy(plan.at[0, g], rbuf.at[q, g], rr.at[q, g]).wait()
 
             @pl.when(jnp.logical_not(from_self))
             def _(q=q):
-                remote(right.at[0], rbuf.at[q], rs.at[0], rr.at[q], sibling).wait_recv()
+                remote(plan.at[0, g], rbuf.at[q, g], rs.at[0, g], rr.at[q, g], sibling).wait_recv()
 
     def sol_send(q, g, d):
         tile = sol.at[2 * x + q, g]
@@ -293,9 +326,7 @@
                 side_in(j, i).wait_recv()
 
     def add_right(q, g):
-        lanes = pl.ds(pl.multiple_of(g * LANES, LANES), LANES)
-        for c in range(2):
-            acc[g, q, :, c * LANES : (c + 1) * LANES] += rbuf[q, :, c, lanes].astype(jnp.float32)
+        acc[g, q] += rbuf[q, g].astype(jnp.float32)
 
     def solve(q, g):
         pending = acc[g, q].astype(jnp.bfloat16)
@@ -315,10 +346,10 @@
         tile = sol.at[j, g]
         return remote(tile, tile, xs.at[j, g, 0], xr.at[j, g], x_dev(-1))
 
-    def relay_row(j):
+    def relay_row(j, groups):
         @pl.when(last)
         def _():
-            for g in range(GROUPS):
+            for g in groups:
                 row_on(j, g).wait_recv()
                 row_on(j, g).start()
 
@@ -347,7 +378,7 @@
             return c
 
         lax.fori_loop(0, x, update, 0)
-        pl.when((g == 0) & (x > 0))(take_right)
+        take_right(g)
         for q in range(2):
             add_right(q, g)
         solve(0, g)
@@ -366,7 +397,6 @@
 
     @pl.when(x == 0)
     def _():
-        take_right()
         lax.fori_loop(0, GROUPS, first, 0)
 
     def relay_step(i):
@@ -377,19 +407,22 @@
 
     relay_step(0)
     for i in range(CHUNKS):
-        if i + 1 < CHUNKS:
+        if i + 1 < RELAYED:
             relay_step(i + 1)
-        if i:
-            relay_row(i - 1)
         if i == 1:
-            @pl.when(begin_mid)
+            relay_row(0, range(GROUPS))
+            pl.when(three)(lambda: relay_step(2))
+        if i == 2:
+            relay_row(1, range(GROUPS - 1))
+        if i < 2:
+            @pl.when(begin_mid & (three if i else jnp.logical_not(three)))
             def _():
                 pl.when(x > 0)(share_right)
                 start_exchange()
 
         @pl.when(early)
         def _(i=i):
-            @pl.when(relay)
+            @pl.when(relay & (three if i >= RELAYED else True))
             def _():
                 pass_on(i).wait_send()
                 keep(i)[1].start()
@@ -398,13 +431,15 @@
 
         @pl.when(needed)
         def _(i=i):
-            hop(i).start()
             for d in (1, 3, 2):
                 y_send(0, i, d).start()
             side_own(i).start()
 
+        if i == 2:
+            relay_row(1, (GROUPS - 1,))
         if i == 0:
             pl.when(early & (x > 0))(lambda: start_lesser(2))
+            pl.when(split & (x > 0))(lambda: start_greater(2))
         elif i == 1:
             pl.when(early & straight)(lambda: start_greater(2))
         else:
@@ -443,17 +478,26 @@
     def _():
         @pl.when(relay)
         def _():
-            for i in range(CHUNKS):
+            for i in range(RELAYED):
                 pass_on(i).wait_send()
                 keep(i)[1].start()
 
+        @pl.when(relay & three)
+        def _():
+            pass_on(RELAYED).wait_send()
+            keep(RELAYED)[1].start()
+
         for i in range(CHUNKS):
             compute_sigma(i)
 
     for i in range(CHUNKS):
         exchange(i)[0].wait_send()
-        pl.when(split)(lambda i=i: pass_out(i).wait_send())
-        pl.when(straight)(lambda i=i: exchange(i)[1].wait_send())
+        if i < RELAYED:
+            pl.when(split)(lambda i=i: pass_out(i).wait_send())
+            pl.when(straight)(lambda i=i: exchange(i)[1].wait_send())
+        else:
+            pl.when(split & three)(lambda i=i: pass_out(i).wait_send())
+            pl.when(jnp.logical_not(split & three))(lambda i=i: exchange(i)[1].wait_send())
         for q in range(2):
             sigma_out(i, q).wait()
 
@@ -478,7 +522,8 @@
                 def _(j=j, i=i):
                     side_send(j, i).wait_send()
     for m in range(2):
-        pl.when(jnp.logical_not(right_self(m)))(lambda m=m: right_send(m).wait_send())
+        for g in range(GROUPS):
+            pl.when(jnp.logical_not(right_self(m)))(lambda m=m, g=g: right_send(m, g).wait_send())
     for q in range(2):
         diag_send(q).wait_send()
     for g in range(GROUPS):
@@ -519,19 +564,21 @@
             pltpu.VMEM((2, SIDE, WIDE), bf16),
             pltpu.VMEM((2, 8, SIDE, WIDE), bf16),
             pltpu.VMEM((2, SIDE, WIDE), bf16),
-            pltpu.VMEM((2, SIDE, 2, SIDE), bf16),
+            pltpu.VMEM((2, GROUPS, SIDE, 2 * LANES), bf16),
             pltpu.VMEM((GROUPS, 2, SIDE, 2 * LANES), f32),
             pltpu.VMEM((8, GROUPS, 2, SIDE, LANES), bf16),
             pltpu.VMEM((2, GROUPS, SIDE, 2, LANES), bf16),
+            pltpu.VMEM((2, SIDE, 2, SIDE), bf16),
+            pltpu.VMEM((2, GROUPS, SIDE, 2 * LANES), bf16),
             dma((CHUNKS, 2)), dma((CHUNKS, 2)), dma((CHUNKS,)), dma((CHUNKS,)), dma((CHUNKS, 2)),
             dma((CHUNKS,)), dma((CHUNKS,)),
             dma((2, CHUNKS, 3)), dma((8, CHUNKS)),
             dma((8, CHUNKS)), dma((8, CHUNKS)),
-            dma((2,)), dma((2,)),
+            dma((2, GROUPS)), dma((2, GROUPS)),
             dma((2,)), dma((2,)), dma((2,)),
             dma((2, GROUPS, 3)), dma((8, GROUPS)),
             dma((2, GROUPS)), dma((2, GROUPS)),
-            dma((CHUNKS, 2)),
+            dma((CHUNKS, 2)), dma((1,)),
         ],
         compiler_params=pltpu.CompilerParams(
             collective_id=0, has_side_effects=True, vmem_limit_bytes=56 * 1024 * 1024

time: 124 us -> 120 us (0.968); the launches traced: 122 us -> 120 us
  Pallas kernels: 118 us -> 116 us
    pallas_call x1, Pallas kernels: 118 us -> 116 us  [on_device(): pl.pallas_call(kernel, out_shape=(jax.ShapeDtypeStruct(lesser.shape, bf16...]
where the time goes in v4:
time: 120 us
  Pallas kernels  116 us (97%)
  local copies, waits for them, and re-layouts  3.51 us (3%)
    pallas_call x1, Pallas kernels, on_device(): pl.pallas_call(kernel, out_shape=(jax.ShapeDtypeStruct(lesser.shape, bf16...  116 us
    unnamed x4, local copies, waits for them, and re-layouts  3.51 us

profile of v4, /device:TPU:23, one launch (start us, length us, event | category | flops | bytes accessed | tf_op | source)
XLA Modules:
  0.0 119.7 jit_solution(18232539189113270638)
XLA Ops:
  0.6 115.5 %second_born.1 = (bf16[2,2,384,384]{3,2,1,0:T(8,128)(2,1)}, bf16[2,384,2,384]{3,2,1,0:T(2,128)(2,1)}) custom-call(s32[3,4,8]{2,1,0:T(4,128)} %bitcast.1, bf16[2,2,384,384]{3,2,1,0:T(8,128)(2,1)} %lesser.1, bf16[2,2,384,384]{3,2,1,0:T(8,128)(2,1)} %greater.1, bf16[2,2,384,384]{3,2,1,0:T(8,128)(2,1)} %diag.1, bf16[2,384,2,384]{3,2,1,0:T(2,128)(2,1)} %right.1), custom_call_target="tpu_custom_call" | custom-call | tf_op jit(solution)/shard_map/second_born/pallas_call | solution.py:552
  116.2 0.0 copy-start
  116.2 2.5 %copy.9 = bf16[2,2,384,384]{3,2,1,0:T(8,128)(2,1)} copy(bf16[2,2,384,384]{3,2,1,0:T(8,128)(2,1)} %get-tuple-element.4) | data formatting | bytes 2359296
  118.7 0.0 copy-done
  118.7 1.0 copy.10
Async XLA Ops:
  116.2 2.5 %copy-start = (bf16[2,384,2,384]{3,2,1,0:T(2,128)(2,1)S(1)}, bf16[2,384,2,384]{3,2,1,0:T(2,128)(2,1)}, u32[]{:S(2)}) copy-start(bf16[2,384,2,384]{3,2,1,0:T(2,128)(2,1)} %get-tuple-element.5) | copy-start | bytes 3538948

commit v5 on v4

--- a/solution.py
+++ b/solution.py
@@ -581,7 +581,7 @@
             dma((CHUNKS, 2)), dma((1,)),
         ],
         compiler_params=pltpu.CompilerParams(
-            collective_id=0, has_side_effects=True, vmem_limit_bytes=56 * 1024 * 1024
+            collective_id=0, has_side_effects=True, vmem_limit_bytes=51 * 1024 * 1024
         ),
         name="second_born",
     )(triples.transpose(2, 0, 1), lesser, greater, diag_inverse, right_side)

time: 120 us -> 119 us (level)
  no operation moved by 1% of the time
where the time goes in v5:
time: 119 us
  Pallas kernels  115 us (97%)
  local copies, waits for them, and re-layouts  2.71 us (2%)
    pallas_call x1, Pallas kernels, on_device(): pl.pallas_call(kernel, out_shape=(jax.ShapeDtypeStruct(lesser.shape, bf16...  115 us
    unnamed x4, local copies, waits for them, and re-layouts  2.71 us

profile of v5, /device:TPU:23, one launch (start us, length us, event | category | flops | bytes accessed | tf_op | source)
XLA Modules:
  0.0 118.6 jit_solution(17805782313428602162)
XLA Ops:
  0.6 0.0 copy-start
  0.6 0.7 copy-done
  1.3 115.2 %second_born.1 = (bf16[2,2,384,384]{3,2,1,0:T(8,128)(2,1)S(1)}, bf16[2,384,2,384]{3,2,1,0:T(2,128)(2,1)S(1)}) custom-call(s32[3,4,8]{2,1,0:T(4,128)S(1)} %bitcast.1, bf16[2,2,384,384]{3,2,1,0:T(8,128)(2,1)} %lesser.1, bf16[2,2,384,384]{3,2,1,0:T(8,128)(2,1)} %greater.1, bf16[2,2,384,384]{3,2,1,0:T(8,128)(2,1)} %diag.1, bf16[2,384,2,384]{3,2,1,0:T(2,128)(2,1)} %right.1), custom_call_target="tpu_custom_call" | custom-call | tf_op jit(solution)/shard_map/second_born/pallas_call | solution.py:552
  116.5 1.0 copy.9
  117.5 1.0 copy.10
Async XLA Ops:
  0.6 0.7 copy-start

commit v6 on v5

--- a/solution.py
+++ b/solution.py
@@ -431,7 +431,7 @@
 
         @pl.when(needed)
         def _(i=i):
-            for d in (1, 3, 2):
+            for d in (2, 1, 3):
                 y_send(0, i, d).start()
             side_own(i).start()
 
@@ -448,7 +448,7 @@
         @pl.when(other_needed)
         def _(i=i):
             hop_in(i).wait_recv()
-            for d in (1, 3, 2):
+            for d in (2, 1, 3):
                 y_send(1, i, d).start()
             side_send(other_col, i).start()
 

time: 119 us -> 119 us (level)
  no operation moved by 1% of the time
where the time goes in v6:
time: 119 us; the launch traced here: 118 us
  Pallas kernels  114 us (96%)
  local copies, waits for them, and re-layouts  2.71 us (2%)
    pallas_call x1, Pallas kernels, on_device(): pl.pallas_call(kernel, out_shape=(jax.ShapeDtypeStruct(lesser.shape, bf16...  114 us
    unnamed x4, local copies, waits for them, and re-layouts  2.71 us

profile of v6, /device:TPU:23, one launch (start us, length us, event | category | flops | bytes accessed | tf_op | source)
XLA Modules:
  0.0 117.7 jit_solution(15149745758389130391)
XLA Ops:
  0.6 0.0 copy-start
  0.6 0.7 copy-done
  1.3 114.4 %second_born.1 = (bf16[2,2,384,384]{3,2,1,0:T(8,128)(2,1)S(1)}, bf16[2,384,2,384]{3,2,1,0:T(2,128)(2,1)S(1)}) custom-call(s32[3,4,8]{2,1,0:T(4,128)S(1)} %bitcast.1, bf16[2,2,384,384]{3,2,1,0:T(8,128)(2,1)} %lesser.1, bf16[2,2,384,384]{3,2,1,0:T(8,128)(2,1)} %greater.1, bf16[2,2,384,384]{3,2,1,0:T(8,128)(2,1)} %diag.1, bf16[2,384,2,384]{3,2,1,0:T(2,128)(2,1)} %right.1), custom_call_target="tpu_custom_call" | custom-call | tf_op jit(solution)/shard_map/second_born/pallas_call | solution.py:552
  115.7 1.0 copy.9
  116.7 1.0 copy.10
Async XLA Ops:
  0.6 0.7 copy-start
